TPU v7x, 32 devices: a whole 2x2x4 slice. The times are simulated.
32 devices in a mesh: seg: 4 (over z), pair: 8 (over y, x, core).
Axes of the slice: x: 2, y: 2, z: 4, core: 2. Of those that a mesh axis runs over, the one named last changes fastest.
Arguments:
- spectra: bfloat16 [4, 2, 2048, 2048], P('seg', None, None, 'pair'), may hold values from -6 to 6
- pair_lists: int32 [32, 2], P('pair'), may hold values from 0 to 15
- pair_counts: int32 [8], P('pair'), may hold values from 1 to 4, as said below
Outputs:
- correlations: float32 [2048, 32, 128], P('seg', 'pair')
Inputs may be any that keep to these rules, and one draw needn't show every extreme that they name: `pair_counts`: some owner uses exactly 4 slots.
All inputs are finite; a program needn't handle non-finite values.
Results may differ from a plain program's by a relative error of at most 0.0003.
Values may be sent and summed in bfloat16 or wider, within the bound.
No kernel may reach another device: no remote copies, remote signals or barrier semaphores. Data moves between devices by JAX's collectives and lax.ppermute only.
A program may use at most 128 MiB of HBM per device.

v0:
```python
import math
import jax
import jax.numpy as jnp
from jax import lax
from jax.sharding import PartitionSpec as P

TILE = 128
LAG = 2048


def stack_weights(linear_re, linear_im, phase_re, phase_im, total_segments):
    weight = (phase_re * phase_re + phase_im * phase_im) / float(total_segments * total_segments)
    return (linear_re * weight, linear_im * weight)


def accumulate(local_spec, group, source_ids, receiver_ids):
    segs_here = local_spec.shape[0]
    band_bins = local_spec.shape[2]
    tiled_spec = local_spec.reshape(segs_here // group, group, 2, band_bins, -1, TILE)

    def one_group(totals, block):
        source_spec = jnp.take(block, source_ids, axis=3).astype(jnp.float32)
        recv_spec = jnp.take(block, receiver_ids, axis=3).astype(jnp.float32)
        cross_re = source_spec[:, 0] * recv_spec[:, 0] + source_spec[:, 1] * recv_spec[:, 1]
        cross_im = source_spec[:, 1] * recv_spec[:, 0] - source_spec[:, 0] * recv_spec[:, 1]
        magnitude = jnp.sqrt(cross_re * cross_re + cross_im * cross_im + 1.0)
        return (
            (
                totals[0] + jnp.sum(cross_re, axis=0),
                totals[1] + jnp.sum(cross_im, axis=0),
                totals[2] + jnp.sum(cross_re / magnitude, axis=0),
                totals[3] + jnp.sum(cross_im / magnitude, axis=0),
            ),
            None,
        )

    zeros = jnp.zeros((band_bins, source_ids.shape[0], TILE), jnp.float32)
    sums, _ = lax.scan(one_group, (zeros, zeros, zeros, zeros), tiled_spec)
    return sums


def body(spectra, pair_lists, pair_counts):
    seg_dev = spectra.shape[0]
    freq_bins = spectra.shape[2]
    n_pair = lax.axis_size("pair")
    n_seg = lax.axis_size("seg")
    seg_index = lax.axis_index("seg")
    most_slots = pair_lists.shape[0]
    total_segments = seg_dev * n_seg
    lists = lax.all_gather(pair_lists, "pair", axis=0, tiled=True)
    source_ids = lists[:, 0]
    receiver_ids = lists[:, 1]
    sub_bins = freq_bins // (n_pair * n_seg)
    bands = lax.all_to_all(spectra, "pair", split_axis=2, concat_axis=3, tiled=True)
    partial_sums = accumulate(bands, seg_dev, source_ids, receiver_ids)
    shares = (
        lax.psum_scatter(partial_sums[0], "seg", scatter_dimension=0, tiled=True),
        lax.psum_scatter(partial_sums[1], "seg", scatter_dimension=0, tiled=True),
        lax.psum_scatter(partial_sums[2], "seg", scatter_dimension=0, tiled=True),
        lax.psum_scatter(partial_sums[3], "seg", scatter_dimension=0, tiled=True),
    )
    block_start = jnp.arange(n_pair, dtype=jnp.int32) * (freq_bins // n_pair) + seg_index * sub_bins
    stack_re, stack_im = stack_weights(shares[0], shares[1], shares[2], shares[3], total_segments)
    stack_re = stack_re.reshape(sub_bins, n_pair, most_slots, TILE)
    stack_im = stack_im.reshape(sub_bins, n_pair, most_slots, TILE)
    owned = (
        lax.all_to_all(stack_re, "pair", split_axis=1, concat_axis=0, tiled=True),
        lax.all_to_all(stack_im, "pair", split_axis=1, concat_axis=0, tiled=True),
    )
    own_bins = sub_bins * n_pair
    row_index = jnp.arange(own_bins, dtype=jnp.int32)
    bin_index = block_start[row_index // sub_bins] + row_index % sub_bins
    owned_re = owned[0].reshape(own_bins, most_slots, TILE)
    owned_im = owned[1].reshape(own_bins, most_slots, TILE)
    live_mask = (jnp.arange(most_slots, dtype=jnp.int32) < pair_counts[0]).astype(jnp.float32)
    owned_re = (owned_re * live_mask[None, :, None]).reshape(own_bins, most_slots * TILE)
    owned_im = (owned_im * live_mask[None, :, None]).reshape(own_bins, most_slots * TILE)
    lag_rows = LAG // n_seg
    lag_offset = jnp.arange(lax.axis_size("seg") * lag_rows, dtype=jnp.int32) - LAG // 2
    product = lag_offset[:, None] * bin_index[None, :] % (2 * freq_bins)
    angles = product.astype(jnp.float32) * jnp.float32(math.pi / freq_bins)
    terms = jnp.dot(
        jnp.cos(angles),
        owned_re,
        precision=lax.Precision.HIGHEST,
        preferred_element_type=jnp.float32,
    )
    terms = terms - jnp.dot(
        jnp.sin(angles),
        owned_im,
        precision=lax.Precision.HIGHEST,
        preferred_element_type=jnp.float32,
    )
    summed = lax.psum_scatter(
        terms * jnp.float32(1.0 / math.sqrt(freq_bins)), "seg", scatter_dimension=0, tiled=True
    )
    return summed.reshape(lag_rows, most_slots, TILE)


def solution(mesh):
    return jax.shard_map(
        body,
        mesh=mesh,
        in_specs=(P("seg", None, None, "pair"), P("pair", None), P("pair")),
        out_specs=P("seg", "pair", None),
        check_vma=False,
    )
```

profile of v0, /device:TPU:0, one launch (start us, length us, event | category | flops | bytes accessed | tf_op | source)
XLA Modules:
  0.0 561.9 jit_solution(8158701286742860428)
XLA Ops:
  6.5 0.0 copy-start.1
  6.5 5.8 %copy.27 = bf16[1,2,2048,256]{3,1,0,2:T(2,128)(2,1)} copy(bf16[1,2,2048,256]{3,2,1,0:T(8,128)(2,1)} %param.5) | data formatting | bytes 4194304 | tf_op args[0]
  12.3 5.2 all-to-all-start
  17.5 0.0 reduce-scatter.10.cloned.1.call-start
  17.5 0.0 copy-done.1
  17.6 29.6 %all-gather = s32[8,4,2]{1,2,0:T(2,128)S(1)} all-gather(s32[1,4,2]{1,2,0:T(2,128)S(1)} %bitcast.100), channel_id=1, replica_groups=mesh['seg'=4,'pair'=8] {'pair'}, dimensions={0}, use_global_device_ids=true | all-gather | bytes 288 | tf_op jit(solution)/shard_map/all_gather | solution.py:50
  47.2 0.1 reshape.246
  47.3 0.0 all-to-all-done
  47.3 1.6 copy.28
  48.9 4.0 copy.29
  52.9 3.0 copy.30
  55.9 3.1 gather_fusion
  59.0 3.0 gather_fusion.1
  62.0 0.0 copy-start
  62.0 2.9 fusion.4
  64.9 0.5 copy-done
  65.4 0.7 fusion.3
  66.1 6.3 %fusion.11 = (f32[256,32,128]{2,0,1:T(8,128)}, f32[256,32,128]{2,0,1:T(8,128)}, f32[256,32,128]{2,0,1:T(8,128)}) fusion(f32[1,2,256,32,128]{4,2,3,1,0:T(8,128)S(1)} %fusion.3, f32[1,2,256,32,128]{4,2,1,3,0:T(8,128)S(1)} %fusion.4), kind=kLoop, calls=%fused_computation.26 | loop fusion | flops 11534336 | bytes 29360128 | tf_op jit(solution)/shard_map/while/body/eval_jaxpr/div | solution.py:31
  72.4 6.4 %fusion.10 = f32[256,32,128]{2,0,1:T(8,128)} fusion(f32[256,32,128]{2,0,1:T(8,128)} %get-tuple-element.22, f32[256,32,128]{2,0,1:T(8,128)} %get-tuple-element.21), kind=kLoop, calls=%fused_computation.25 | loop fusion | flops 5242880 | bytes 12582912 | tf_op jit(solution)/shard_map/while/body/eval_jaxpr/div | solution.py:32
  78.9 0.0 reduce-scatter.10.cloned.1.call-update
  78.9 0.0 reduce-scatter.12.cloned.1.call-start
  78.9 0.7 reduce-scatter.12.cloned.1.call-update
  79.6 0.0 reduce-scatter.6.cloned.1.call-start
  79.7 0.7 reduce-scatter.6.cloned.1.call-update
  80.4 0.0 reduce-scatter.8.cloned.1.call-start
  80.4 0.5 reduce-scatter.8.cloned.1.call-update
  81.0 74.2 %reduce-scatter.10.cloned.1.call-done = f32[64,32,128]{2,0,1:T(8,128)} async-done(((f32[256,32,128]{2,0,1:T(8,128)}), f32[64,32,128]{2,0,1:T(8,128)}) %reduce-scatter.10.cloned.1.call-update) | async-done | bytes 1048592 | tf_op jit(solution)/shard_map/reduce_scatter | solution.py:60
  155.2 79.7 %reduce-scatter.12.cloned.1.call-done = f32[64,32,128]{2,0,1:T(8,128)} async-done(((f32[256,32,128]{2,0,1:T(8,128)}), f32[64,32,128]{2,0,1:T(8,128)}) %reduce-scatter.12.cloned.1.call-update) | async-done | bytes 1048592 | tf_op jit(solution)/shard_map/reduce_scatter | solution.py:58
  234.9 79.6 %reduce-scatter.6.cloned.1.call-done = f32[64,32,128]{2,0,1:T(8,128)} async-done(((f32[256,32,128]{2,0,1:T(8,128)}), f32[64,32,128]{2,0,1:T(8,128)}) %reduce-scatter.6.cloned.1.call-update) | async-done | bytes 1048592 | tf_op jit(solution)/shard_map/reduce_scatter | solution.py:57
  314.5 79.6 %reduce-scatter.8.cloned.1.call-done = f32[64,32,128]{2,0,1:T(8,128)} async-done(((f32[256,32,128]{2,0,1:T(8,128)}), f32[64,32,128]{2,0,1:T(8,128)}) %reduce-scatter.8.cloned.1.call-update) | async-done | bytes 1048592 | tf_op jit(solution)/shard_map/reduce_scatter | solution.py:59
  394.1 2.6 fusion.23
  396.7 1.6 copy.38
  398.3 3.6 all-to-all-start.2
  402.7 0.7 fusion.38
  403.3 0.1 broadcast_bitcast_fusion
  403.4 1.6 copy.37
  405.0 12.4 %all-to-all-done.2 = f32[64,8,4,128]{3,2,0,1:T(4,128)S(1)} async-done(((f32[64,8,4,128]{3,2,0,1:T(4,128)}), f32[64,8,4,128]{3,2,0,1:T(4,128)S(1)}, u32[]{:S(2)}, u32[]{:S(2)}) %all-to-all-start.2) | async-done | bytes 1048608 | tf_op jit(solution)/shard_map/all_to_all | solution.py:68
  417.4 3.6 all-to-all-start.1
  420.9 0.2 reduce-scatter.14.cloned.1.call-start
  421.2 4.3 compare_select_fusion.1
  425.5 0.6 fusion.24
  426.1 23.5 %fusion.8 = f32[2048,512]{1,0:T(8,128)} fusion(s32[512]{0:T(512)S(1)} %fusion.24, s32[2048]{0:T(1024)S(1)} %iota_add_fusion, f32[64,8,4,128]{3,2,1,0:T(4,128)S(1)} %bitcast.97, f32[512]{0:T(512)S(1)} %broadcast_bitcast_fusion), kind=kOutput, calls=%fused_computation.22 | convolution fusion | flops 6457393152 | bytes 5255168 | tf_op jit(solution)/shard_map/dot_general | solution.py:88
  449.6 0.0 all-to-all-done.1
  449.6 25.5 %subtract_multiply_fusion = f32[2048,512]{1,0:T(8,128)} fusion(f32[2048,512]{1,0:T(8,128)} %fusion.8, s32[512]{0:T(512)S(1)} %fusion.24, s32[2048]{0:T(1024)S(1)} %iota_add_fusion, f32[64,8,4,128]{3,2,1,0:T(4,128)S(1)} %bitcast.98, f32[512]{0:T(512)S(1)} %broadcast_bitcast_fusion), kind=kOutput, calls=%fused_computation.21 | convolution fusion | flops 6459490304 | bytes 9449472 | tf_op jit(solution)/shard_map/dot_general | solution.py:82
  475.1 0.0 reduce-scatter.14.cloned.1.call-update
  475.2 77.7 %reduce-scatter.14.cloned.1.call-done = f32[512,512]{1,0:T(8,128)} async-done(((f32[2048,512]{1,0:T(8,128)}), f32[512,512]{1,0:T(8,128)}) %reduce-scatter.14.cloned.1.call-update) | async-done | bytes 1048592 | tf_op jit(solution)/shard_map/reduce_scatter | solution.py:94
  552.8 2.5 reshape.186
  (7 shorter events, 0.1 us)
Async XLA Ops:
  6.5 11.0 %copy-start.1 = (s32[4,2]{0,1:T(2,128)S(1)}, s32[4,2]{0,1:T(2,128)}, u32[]{:S(2)}) copy-start(s32[4,2]{0,1:T(2,128)} %param.6) | copy-start | bytes 100
  12.3 35.0 %all-to-all-start = ((bf16[1,2,2048,256]{3,1,0,2:T(2,128)(2,1)}), bf16[1,2,2048,256]{3,1,0,2:T(2,128)(2,1)S(1)}, u32[]{:S(2)}, u32[]{:S(2)}) async-start(bf16[1,2,2048,256]{3,1,0,2:T(2,128)(2,1)} %copy.27), calls=%async_computation | async-start | bytes 4194304 | tf_op jit(solution)/shard_map/all_to_all | solution.py:54
  17.5 137.7 %reduce-scatter.10.cloned.1.call-start = ((), (), s32[]{:S(2)}) async-start(), calls=%async_computation.10 | async-start | bytes 5242880 | tf_op jit(solution)/shard_map/reduce_scatter | solution.py:60
  62.0 3.4 copy-start
  78.9 156.0 %reduce-scatter.12.cloned.1.call-start = ((), (), s32[]{:S(2)}) async-start(), calls=%async_computation.11 | async-start | bytes 5242880 | tf_op jit(solution)/shard_map/reduce_scatter | solution.py:58
  79.6 234.8 %reduce-scatter.6.cloned.1.call-start = ((), (), s32[]{:S(2)}) async-start(), calls=%async_computation.8 | async-start | bytes 5242880 | tf_op jit(solution)/shard_map/reduce_scatter | solution.py:57
  80.4 313.7 %reduce-scatter.8.cloned.1.call-start = ((), (), s32[]{:S(2)}) async-start(), calls=%async_computation.9 | async-start | bytes 5242880 | tf_op jit(solution)/shard_map/reduce_scatter | solution.py:59
  398.3 19.1 %all-to-all-start.2 = ((f32[64,8,4,128]{3,2,0,1:T(4,128)}), f32[64,8,4,128]{3,2,0,1:T(4,128)S(1)}, u32[]{:S(2)}, u32[]{:S(2)}) async-start(f32[64,8,4,128]{3,2,0,1:T(4,128)} %copy.38), calls=%async_computation.6 | async-start | bytes 2097152 | tf_op jit(solution)/shard_map/all_to_all | solution.py:68
  417.4 32.3 %all-to-all-start.1 = ((f32[64,8,4,128]{3,2,0,1:T(4,128)}), f32[64,8,4,128]{3,2,0,1:T(4,128)S(1)}, u32[]{:S(2)}, u32[]{:S(2)}) async-start(f32[64,8,4,128]{3,2,0,1:T(4,128)} %copy.37), calls=%async_computation.4 | async-start | bytes 2097152 | tf_op jit(solution)/shard_map/all_to_all | solution.py:67
  420.9 131.9 %reduce-scatter.14.cloned.1.call-start = ((), (), s32[]{:S(2)}) async-start(), calls=%async_computation.12 | async-start | bytes 5242880 | tf_op jit(solution)/shard_map/reduce_scatter | solution.py:94
Sparse Core Ops, SparseCore 0:
  79.0 76.1 reduce-scatter.9
  157.6 77.2 reduce-scatter.11
  237.2 77.2 reduce-scatter.5
  316.7 77.2 reduce-scatter.7
  475.3 77.5 reduce-scatter.13
where the time goes:
time: 563 us; the launch traced here: 562 us
  waiting for transfers between devices  405 us (72%)
  matrix products  49 us (9%)
  blocking collectives  29.6 us (5%)
  local copies, waits for them, and re-layouts  27.6 us (5%)
  other arithmetic  23.9 us (4%)
  between operations  13.9 us (2%)
  starting transfers between devices  12.7 us (2%)
    reduce_scatter x1, waiting for transfers between devices, body(): lax.psum_scatter(partial_sums[1], 'seg', scatter_dimension=0, tiled=True)  79.7 us
    reduce_scatter x1, waiting for transfers between devices, body(): lax.psum_scatter(partial_sums[0], 'seg', scatter_dimension=0, tiled=True)  79.6 us
    reduce_scatter x1, waiting for transfers between devices, body(): lax.psum_scatter(partial_sums[2], 'seg', scatter_dimension=0, tiled=True)  79.6 us
    reduce_scatter x1, waiting for transfers between devices, body(): lax.psum_scatter(terms * jnp.float32(1.0 / math.sqrt(freq_bins)), 'seg',...  77.7 us
    reduce_scatter x1, waiting for transfers between devices, body(): lax.psum_scatter(partial_sums[3], 'seg', scatter_dimension=0, tiled=True)  74.2 us
    all_gather x1, blocking collectives, body(): lists = lax.all_gather(pair_lists, 'pair', axis=0, tiled=True)  29.6 us
    dot_general x1, matrix products, body(): jnp.dot(jnp.cos(angles), owned_re, precision=lax.Precision.HIGHEST, prefe...  25.5 us
    dot_general x1, matrix products, body(): jnp.dot(jnp.sin(angles), owned_im, precision=lax.Precision.HIGHEST, prefe...  23.5 us
  transfers between devices with their start and end apart: 8, of which 6 were waited for; matrix products, arithmetic and copies ran while one was open for 6% of the time, Pallas kernels for 0%

commit v1 on v0

--- a/solution.py
+++ b/solution.py
@@ -65,7 +65,12 @@
     stack_im = stack_im.reshape(sub_bins, n_pair, most_slots, TILE)
     owned = (
         lax.all_to_all(stack_re, "pair", split_axis=1, concat_axis=0, tiled=True),
-        lax.all_to_all(stack_im, "pair", split_axis=1, concat_axis=0, tiled=True),
+        jnp.concatenate(
+            lax.all_to_all(
+                jnp.stack(jnp.split(stack_im, lax.axis_size("pair"), axis=1)), "pair", 0, 0
+            ),
+            axis=0,
+        ),
     )
     own_bins = sub_bins * n_pair
     row_index = jnp.arange(own_bins, dtype=jnp.int32)

time: 563 us -> 567 us (level)
  no operation moved by 1% of the time
where the time goes in v1:
time: 567 us; the launch traced here: 566 us
  waiting for transfers between devices  405 us (71%)
  matrix products  49 us (9%)
  local copies, waits for them, and re-layouts  31.9 us (6%)
  blocking collectives  29.6 us (5%)
  other arithmetic  23.9 us (4%)
  between operations  13.9 us (2%)
  starting transfers between devices  12.7 us (2%)
    reduce_scatter x1, waiting for transfers between devices, body(): lax.psum_scatter(partial_sums[1], 'seg', scatter_dimension=0, tiled=True)  79.7 us
    reduce_scatter x1, waiting for transfers between devices, body(): lax.psum_scatter(partial_sums[0], 'seg', scatter_dimension=0, tiled=True)  79.6 us
    reduce_scatter x1, waiting for transfers between devices, body(): lax.psum_scatter(partial_sums[2], 'seg', scatter_dimension=0, tiled=True)  79.6 us
    reduce_scatter x1, waiting for transfers between devices, body(): lax.psum_scatter(terms * jnp.float32(1.0 / math.sqrt(freq_bins)), 'seg',...  77.7 us
    reduce_scatter x1, waiting for transfers between devices, body(): lax.psum_scatter(partial_sums[3], 'seg', scatter_dimension=0, tiled=True)  74.2 us
    all_gather x1, blocking collectives, body(): lists = lax.all_gather(pair_lists, 'pair', axis=0, tiled=True)  29.6 us
    dot_general x1, matrix products, body(): jnp.dot(jnp.cos(angles), owned_re, precision=lax.Precision.HIGHEST, prefe...  25.5 us
    dot_general x1, matrix products, body(): jnp.dot(jnp.sin(angles), owned_im, precision=lax.Precision.HIGHEST, prefe...  23.5 us
  transfers between devices with their start and end apart: 8, of which 6 were waited for; matrix products, arithmetic and copies ran while one was open for 6% of the time, Pallas kernels for 0%

profile of v1, /device:TPU:0, one launch (start us, length us, event | category | flops | bytes accessed | tf_op | source)
XLA Modules:
  0.0 566.3 jit_solution(10512179582923542442)
XLA Ops:
  6.5 5.8 %copy.34 = bf16[1,2,2048,256]{3,1,0,2:T(2,128)(2,1)} copy(bf16[1,2,2048,256]{3,2,1,0:T(8,128)(2,1)} %param.5) | data formatting | bytes 4194304 | tf_op args[0]
  12.3 5.2 all-to-all-start
  17.5 0.0 reduce-scatter.10.cloned.1.call-start
  17.6 29.6 %all-gather = s32[8,4,2]{1,2,0:T(2,128)S(1)} all-gather(s32[1,4,2]{1,2,0:T(2,128)S(1)} %bitcast.136), channel_id=1, replica_groups=mesh['seg'=4,'pair'=8] {'pair'}, dimensions={0}, use_global_device_ids=true | all-gather | bytes 288 | tf_op jit(solution)/shard_map/all_gather | solution.py:50
  47.2 0.1 reshape.241
  47.3 1.6 copy.35
  48.9 4.0 copy.36
  52.9 3.0 copy.37
  55.9 3.1 gather_fusion
  59.0 3.0 gather_fusion.1
  62.0 2.9 fusion.4
  64.9 0.5 copy-done
  65.4 0.7 fusion.3
  66.1 6.3 %fusion.11 = (f32[256,32,128]{2,0,1:T(8,128)}, f32[256,32,128]{2,0,1:T(8,128)}, f32[256,32,128]{2,0,1:T(8,128)}) fusion(f32[1,2,256,32,128]{4,2,3,1,0:T(8,128)S(1)} %fusion.3, f32[1,2,256,32,128]{4,2,1,3,0:T(8,128)S(1)} %fusion.4), kind=kLoop, calls=%fused_computation.26 | loop fusion | flops 11534336 | bytes 29360128 | tf_op jit(solution)/shard_map/while/body/eval_jaxpr/div | solution.py:31
  72.4 6.4 %fusion.10 = f32[256,32,128]{2,0,1:T(8,128)} fusion(f32[256,32,128]{2,0,1:T(8,128)} %get-tuple-element.22, f32[256,32,128]{2,0,1:T(8,128)} %get-tuple-element.21), kind=kLoop, calls=%fused_computation.25 | loop fusion | flops 5242880 | bytes 12582912 | tf_op jit(solution)/shard_map/while/body/eval_jaxpr/div | solution.py:32
  78.9 0.0 reduce-scatter.12.cloned.1.call-start
  78.9 0.7 reduce-scatter.12.cloned.1.call-update
  79.6 0.0 reduce-scatter.6.cloned.1.call-start
  79.7 0.7 reduce-scatter.6.cloned.1.call-update
  80.4 0.0 reduce-scatter.8.cloned.1.call-start
  80.4 0.5 reduce-scatter.8.cloned.1.call-update
  81.0 74.2 %reduce-scatter.10.cloned.1.call-done = f32[64,32,128]{2,0,1:T(8,128)} async-done(((f32[256,32,128]{2,0,1:T(8,128)}), f32[64,32,128]{2,0,1:T(8,128)}) %reduce-scatter.10.cloned.1.call-update) | async-done | bytes 1048592 | tf_op jit(solution)/shard_map/reduce_scatter | solution.py:60
  155.2 79.7 %reduce-scatter.12.cloned.1.call-done = f32[64,32,128]{2,0,1:T(8,128)} async-done(((f32[256,32,128]{2,0,1:T(8,128)}), f32[64,32,128]{2,0,1:T(8,128)}) %reduce-scatter.12.cloned.1.call-update) | async-done | bytes 1048592 | tf_op jit(solution)/shard_map/reduce_scatter | solution.py:58
  234.9 79.6 %reduce-scatter.6.cloned.1.call-done = f32[64,32,128]{2,0,1:T(8,128)} async-done(((f32[256,32,128]{2,0,1:T(8,128)}), f32[64,32,128]{2,0,1:T(8,128)}) %reduce-scatter.6.cloned.1.call-update) | async-done | bytes 1048592 | tf_op jit(solution)/shard_map/reduce_scatter | solution.py:57
  314.5 79.6 %reduce-scatter.8.cloned.1.call-done = f32[64,32,128]{2,0,1:T(8,128)} async-done(((f32[256,32,128]{2,0,1:T(8,128)}), f32[64,32,128]{2,0,1:T(8,128)}) %reduce-scatter.8.cloned.1.call-update) | async-done | bytes 1048592 | tf_op jit(solution)/shard_map/reduce_scatter | solution.py:59
  394.1 2.6 fusion.23
  396.7 0.7 fusion.31
  397.3 0.7 fusion.30
  398.0 0.7 fusion.29
  398.7 0.7 fusion.28
  399.3 0.7 fusion.27
  400.0 0.7 fusion.26
  400.7 0.7 fusion.25
  401.3 0.7 fusion.24
  402.0 3.6 all-to-all-start.2
  406.3 0.7 fusion.46
  407.0 0.1 broadcast_bitcast_fusion
  407.0 1.6 copy.44
  408.7 12.4 %all-to-all-done.2 = f32[8,64,1,4,128]{4,1,3,2,0:T(8,128)S(1)} async-done(((f32[8,64,1,4,128]{4,1,3,2,0:T(8,128)}), f32[8,64,1,4,128]{4,1,3,2,0:T(8,128)S(1)}, u32[]{:S(2)}, u32[]{:S(2)}) %all-to-all-start.2) | async-done | bytes 1048608 | tf_op jit(solution)/shard_map/all_to_all | solution.py:69
  421.0 3.6 all-to-all-start.1
  424.6 0.2 reduce-scatter.14.cloned.1.call-start
  424.8 4.3 compare_select_fusion.1
  429.1 0.6 fusion.32
  429.8 0.7 copy.45
  430.5 23.5 %fusion.8 = f32[2048,512]{1,0:T(8,128)} fusion(s32[512]{0:T(512)S(1)} %fusion.32, s32[2048]{0:T(1024)S(1)} %iota_add_fusion, f32[64,8,4,128]{3,2,1,0:T(4,128)S(1)} %bitcast.134, f32[512]{0:T(512)S(1)} %broadcast_bitcast_fusion), kind=kOutput, calls=%fused_computation.22 | convolution fusion | flops 6457393152 | bytes 5255168 | tf_op jit(solution)/shard_map/dot_general | solution.py:93
  454.0 25.5 %subtract_multiply_fusion = f32[2048,512]{1,0:T(8,128)} fusion(f32[2048,512]{1,0:T(8,128)} %fusion.8, s32[512]{0:T(512)S(1)} %fusion.32, s32[2048]{0:T(1024)S(1)} %iota_add_fusion, f32[64,8,4,128]{3,2,1,0:T(4,128)S(1)} %bitcast.133, f32[512]{0:T(512)S(1)} %broadcast_bitcast_fusion), kind=kOutput, calls=%fused_computation.21 | convolution fusion | flops 6459490304 | bytes 9449472 | tf_op jit(solution)/shard_map/dot_general | solution.py:87
  479.5 77.7 %reduce-scatter.14.cloned.1.call-done = f32[512,512]{1,0:T(8,128)} async-done(((f32[2048,512]{1,0:T(8,128)}), f32[512,512]{1,0:T(8,128)}) %reduce-scatter.14.cloned.1.call-update) | async-done | bytes 1048592 | tf_op jit(solution)/shard_map/reduce_scatter | solution.py:99
  557.2 2.5 reshape.181
  (14 shorter events, 0.1 us)
Async XLA Ops:
  6.5 11.0 %copy-start.1 = (s32[4,2]{0,1:T(2,128)S(1)}, s32[4,2]{0,1:T(2,128)}, u32[]{:S(2)}) copy-start(s32[4,2]{0,1:T(2,128)} %param.6) | copy-start | bytes 100
  12.3 35.0 %all-to-all-start = ((bf16[1,2,2048,256]{3,1,0,2:T(2,128)(2,1)}), bf16[1,2,2048,256]{3,1,0,2:T(2,128)(2,1)S(1)}, u32[]{:S(2)}, u32[]{:S(2)}) async-start(bf16[1,2,2048,256]{3,1,0,2:T(2,128)(2,1)} %copy.34), calls=%async_computation | async-start | bytes 4194304 | tf_op jit(solution)/shard_map/all_to_all | solution.py:54
  17.5 137.7 %reduce-scatter.10.cloned.1.call-start = ((), (), s32[]{:S(2)}) async-start(), calls=%async_computation.10 | async-start | bytes 5242880 | tf_op jit(solution)/shard_map/reduce_scatter | solution.py:60
  62.0 3.4 copy-start
  78.9 156.0 %reduce-scatter.12.cloned.1.call-start = ((), (), s32[]{:S(2)}) async-start(), calls=%async_computation.11 | async-start | bytes 5242880 | tf_op jit(solution)/shard_map/reduce_scatter | solution.py:58
  79.6 234.8 %reduce-scatter.6.cloned.1.call-start = ((), (), s32[]{:S(2)}) async-start(), calls=%async_computation.8 | async-start | bytes 5242880 | tf_op jit(solution)/shard_map/reduce_scatter | solution.py:57
  80.4 313.7 %reduce-scatter.8.cloned.1.call-start = ((), (), s32[]{:S(2)}) async-start(), calls=%async_computation.9 | async-start | bytes 5242880 | tf_op jit(solution)/shard_map/reduce_scatter | solution.py:59
  402.0 19.1 %all-to-all-start.2 = ((f32[8,64,1,4,128]{4,1,3,2,0:T(8,128)}), f32[8,64,1,4,128]{4,1,3,2,0:T(8,128)S(1)}, u32[]{:S(2)}, u32[]{:S(2)}) async-start(f32[8,64,1,4,128]{4,1,3,2,0:T(8,128)} %fusion.24), calls=%async_computation.6 | async-start | bytes 2097152 | tf_op jit(solution)/shard_map/all_to_all | solution.py:69
  421.0 32.9 %all-to-all-start.1 = ((f32[64,8,4,128]{3,2,0,1:T(4,128)}), f32[64,8,4,128]{3,2,0,1:T(4,128)S(1)}, u32[]{:S(2)}, u32[]{:S(2)}) async-start(f32[64,8,4,128]{3,2,0,1:T(4,128)} %copy.44), calls=%async_computation.4 | async-start | bytes 2097152 | tf_op jit(solution)/shard_map/all_to_all | solution.py:67
  424.6 132.6 %reduce-scatter.14.cloned.1.call-start = ((), (), s32[]{:S(2)}) async-start(), calls=%async_computation.12 | async-start | bytes 5242880 | tf_op jit(solution)/shard_map/reduce_scatter | solution.py:99
Sparse Core Ops, SparseCore 0:
  79.0 76.1 reduce-scatter.9
  157.6 77.2 reduce-scatter.11
  237.2 77.2 reduce-scatter.5
  316.7 77.2 reduce-scatter.7
  479.6 77.5 reduce-scatter.13
